TPU v7x, 32 devices: a whole 2x2x4 slice. The times are simulated.
32 devices in a mesh: dp: 2 (over x), row: 4 (over z), col: 4 (over y, core).
Axes of the slice: x: 2, y: 2, z: 4, core: 2. Of those that a mesh axis runs over, the one named last changes fastest.
Arguments:
- layer_input: bfloat16 [4096, 1024], P(('dp', 'col'), 'row'), may hold values from -40 to 40
- segment_ids: int32 [2, 2048], P('dp'), may hold values from 0 to 7, never falling along the last dimension, each value on 1 to 512 neighbouring positions
- norm1_gain: float32 [1024], P('row'), may hold values from 0.1 to 1.9
- in_weight: bfloat16 [1024, 3, 1024], P('row', None, 'col'), may hold values from -0.1875 to 0.1875
- conv_weight: float32 [3, 1024], P(None, 'col'), may hold values from -3 to 3
- out_weight: bfloat16 [1024, 1024], P('col', 'row'), may hold values from -0.1875 to 0.1875
- norm2_gain: float32 [1024], P('row'), may hold values from 0.1 to 1.9
- gate_up_weight: bfloat16 [1024, 2, 4608], P('row', None, 'col'), may hold values from -0.1875 to 0.1875
- down_weight: bfloat16 [4608, 1024], P('col', 'row'), may hold values from -0.09375 to 0.09375
- cotangent: bfloat16 [4096, 1024], P(('dp', 'col'), 'row'), may hold values from -6 to 6
Outputs:
- block_out: bfloat16 [4096, 1024], P(('dp', 'col'), 'row')
- grad_x: float32 [4096, 1024], P(('dp', 'col'), 'row')
- grad_norm1: float32 [1024], P('row')
- grad_in: float32 [1024, 3, 1024], P('row', None, 'col')
- grad_conv: float32 [3, 1024], P(None, 'col')
- grad_out: float32 [1024, 1024], P('col', 'row')
- grad_norm2: float32 [1024], P('row')
- grad_gate_up: float32 [1024, 2, 4608], P('row', None, 'col')
- grad_down: float32 [4608, 1024], P('col', 'row')
Inputs may be any that keep to these rules, and one draw needn't show every extreme that they name: `segment_ids`: within each sequence the ids never fall; each document has 1 to 512 tokens and one has exactly that many.
All inputs are finite; a program needn't handle non-finite values.
Results may differ from a plain program's by a relative error of at most 0.0092.
Values may be sent and summed in bfloat16 or wider, within the bound.
A program may use at most 128 MiB of HBM per device.

v0:
```python
import jax
import jax.numpy as jnp
from jax import lax
from jax.sharding import PartitionSpec as P

D = 1024
EPSILON = 1e-05


def passed_along(block, axis, distance):
    devices = range(lax.axis_size(axis))
    route = [(i - distance, i) for i in devices if i - distance in devices]
    return lax.ppermute(block, axis, route)


def spread_cols(local):
    return lax.all_gather(local, "col", axis=0, tiled=True)


def spread_rows(local):
    return lax.all_gather(local, "row", axis=0, tiled=True)


def summed_rows(whole_rows, weight, einsum_form, row_count):

    def term(row_start, count_rows):
        return jnp.einsum(einsum_form, whole_rows, weight, preferred_element_type=jnp.float32)

    return lax.psum_scatter(
        term(jnp.int32(0), row_count * lax.axis_size("row")), "row", scatter_dimension=0, tiled=True
    )


def summed_cols(whole_rows, weight, einsum_form, row_count):

    def term(row_start, count_rows):
        return jnp.einsum(einsum_form, whole_rows, weight, preferred_element_type=jnp.float32)

    return lax.psum_scatter(
        term(jnp.int32(0), row_count * lax.axis_size("col")), "col", scatter_dimension=0, tiled=True
    )


def norm_scale(inputs):
    squares = lax.psum(jnp.sum(inputs * inputs, axis=1), "row")
    return lax.rsqrt(squares / D + EPSILON)


def norm_back(inputs, scales, gains, grads):
    gained = gains * grads
    dots = lax.psum(jnp.sum(gained * inputs, axis=1), "row") / D
    return scales[:, None] * gained - inputs * (scales * scales * scales)[:, None] * dots[:, None]


def on_device(
    layer_input,
    segment_ids,
    norm1_gain,
    in_weight,
    conv_weight,
    out_weight,
    norm2_gain,
    gate_up_weight,
    down_weight,
    cotangent,
):
    seq_len = segment_ids.shape[1]
    row_tokens = seq_len // lax.axis_size("row")
    col_tokens = seq_len // lax.axis_size("col")
    row_feats = layer_input.shape[1]
    col_feats = conv_weight.shape[1]
    row_place = lax.axis_index("row")
    col_place = lax.axis_index("col")
    x_wide = layer_input.astype(jnp.float32)
    scale_one = norm_scale(x_wide)
    x_normed = (x_wide * scale_one[:, None] * norm1_gain).astype(jnp.bfloat16)
    normed_all = spread_cols(x_normed)
    mixed_in = summed_rows(normed_all, in_weight, "td,dkf->tkf", row_tokens)
    b_gate = mixed_in[:, 0]
    c_gate = mixed_in[:, 1]
    v_part = mixed_in[:, 2]
    gated_in = b_gate * v_part
    seg_padded = jnp.concatenate([jnp.full((2,), -1, jnp.int32), segment_ids[0]])
    seg_ext = lax.dynamic_slice_in_dim(seg_padded, row_place * row_tokens, row_tokens + 2, 0)
    seg_own = seg_ext[2:]
    mask_one = (seg_ext[1 : row_tokens + 1] == seg_own).astype(jnp.float32)[:, None]
    mask_two = (seg_ext[0:row_tokens] == seg_own).astype(jnp.float32)[:, None]
    prev_rows = passed_along(gated_in[row_tokens - 2 :], "row", 1)
    extended = jnp.concatenate([prev_rows, gated_in])
    prev_one = extended[1 : row_tokens + 1]
    prev_two = extended[0:row_tokens]
    conv_out = (
        conv_weight[0] * gated_in
        + conv_weight[1] * mask_one * prev_one
        + conv_weight[2] * mask_two * prev_two
    )
    mixer_out = (c_gate * conv_out).astype(jnp.bfloat16)
    mixer_all = spread_rows(mixer_out)
    resid = x_wide + summed_cols(mixer_all, out_weight, "tf,fd->td", col_tokens)
    scale_two = norm_scale(resid)
    h_normed = (resid * scale_two[:, None] * norm2_gain).astype(jnp.bfloat16)
    hn_all = spread_cols(h_normed)
    gate_up = summed_rows(hn_all, gate_up_weight, "td,dkf->tkf", row_tokens)
    gate_pre = gate_up[:, 0]
    up_pre = gate_up[:, 1]
    gate_sig = jax.nn.sigmoid(gate_pre)
    hidden = (gate_pre * gate_sig * up_pre).astype(jnp.bfloat16)
    hidden_all = spread_rows(hidden)
    block_out = (resid + summed_cols(hidden_all, down_weight, "tf,fd->td", col_tokens)).astype(
        jnp.bfloat16
    )
    cot_all = spread_cols(cotangent)
    grad_hidden = summed_rows(cot_all, down_weight, "td,fd->tf", row_tokens)
    grad_down = jnp.einsum("tf,td->fd", hidden_all, cot_all, preferred_element_type=jnp.float32)
    grad_gu = jnp.stack(
        [
            grad_hidden * up_pre * gate_sig * (1.0 + gate_pre * (1.0 - gate_sig)),
            grad_hidden * gate_pre * gate_sig,
        ],
        axis=1,
    ).astype(jnp.bfloat16)
    ggu_all = spread_rows(grad_gu)
    grad_hn = summed_cols(ggu_all, gate_up_weight, "tkf,dkf->td", col_tokens)
    grad_gate_up = jnp.einsum("td,tkf->dkf", hn_all, ggu_all, preferred_element_type=jnp.float32)
    norm2_part = jnp.sum(grad_hn * resid * scale_two[:, None], axis=0)
    grad_resid = cotangent.astype(jnp.float32) + norm_back(resid, scale_two, norm2_gain, grad_hn)
    resid_cast = grad_resid.astype(jnp.bfloat16)
    rcast_all = spread_cols(resid_cast)
    grad_mixer = summed_rows(rcast_all, out_weight, "td,fd->tf", row_tokens)
    grad_out = jnp.einsum("tf,td->fd", mixer_all, rcast_all, preferred_element_type=jnp.float32)
    grad_conv_out = grad_mixer * c_gate
    grad_c = grad_mixer * conv_out
    conv_part = jnp.stack(
        [
            jnp.sum(grad_conv_out * gated_in, axis=0),
            jnp.sum(grad_conv_out * mask_one * prev_one, axis=0),
            jnp.sum(grad_conv_out * mask_two * prev_two, axis=0),
        ]
    )
    later_one = conv_weight[1] * mask_one * grad_conv_out
    later_two = conv_weight[2] * mask_two * grad_conv_out
    next_rows = passed_along(jnp.stack([later_one[0:2], later_two[0:2]]), "row", -1)
    grad_gated = (
        conv_weight[0] * grad_conv_out
        + jnp.concatenate([later_one[1:], next_rows[0, 0:1]])
        + jnp.concatenate([later_two[2:], next_rows[1]])
    )
    grad_mixed = jnp.stack([grad_gated * v_part, grad_c, grad_gated * b_gate], axis=1).astype(
        jnp.bfloat16
    )
    gmix_all = spread_rows(grad_mixed)
    grad_xn = summed_cols(gmix_all, in_weight, "tkf,dkf->td", col_tokens)
    grad_in = jnp.einsum("td,tkf->dkf", normed_all, gmix_all, preferred_element_type=jnp.float32)
    norm1_part = jnp.sum(grad_xn * x_wide * scale_one[:, None], axis=0)
    grad_x = grad_resid + norm_back(x_wide, scale_one, norm1_gain, grad_xn)
    conv_padded = lax.dynamic_update_slice_in_dim(
        jnp.zeros((3, D), jnp.float32), conv_part, col_place * col_feats, 1
    )
    gain_padded = lax.dynamic_update_slice_in_dim(
        jnp.zeros((2, D), jnp.float32),
        jnp.stack([norm1_part, norm2_part]),
        row_place * row_feats,
        1,
    )
    conv_total, gain_total = lax.psum((conv_padded, gain_padded), ("row", "col"))
    conv_own = lax.dynamic_slice_in_dim(conv_total, col_place * col_feats, col_feats, 1)
    gain_own = lax.dynamic_slice_in_dim(gain_total, row_place * row_feats, row_feats, 1)
    grad_in, grad_out, grad_gate_up, grad_down, conv_own, gain_own = lax.psum(
        (grad_in, grad_out, grad_gate_up, grad_down, conv_own, gain_own), "dp"
    )
    return (
        block_out,
        grad_x,
        gain_own[0],
        grad_in,
        conv_own,
        grad_out,
        gain_own[1],
        grad_gate_up,
        grad_down,
    )


def solution(mesh):
    return jax.shard_map(
        on_device,
        mesh=mesh,
        in_specs=(
            P(("dp", "col"), "row"),
            P("dp", None),
            P("row"),
            P("row", None, "col"),
            P(None, "col"),
            P("col", "row"),
            P("row"),
            P("row", None, "col"),
            P("col", "row"),
            P(("dp", "col"), "row"),
        ),
        out_specs=(
            P(("dp", "col"), "row"),
            P(("dp", "col"), "row"),
            P("row"),
            P("row", None, "col"),
            P(None, "col"),
            P("col", "row"),
            P("row"),
            P("row", None, "col"),
            P("col", "row"),
        ),
        check_vma=False,
    )
```

profile of v0, /device:TPU:0, one launch (start us, length us, event | category | flops | bytes accessed | tf_op | source)
XLA Modules:
  0.0 1381.3 jit_solution(11055244738655063298)
XLA Ops:
  7.2 1.2 fusion.15
  8.4 13.5 psum.84
  21.9 0.6 multiply_multiply_fusion.4
  22.5 1.8 fusion.17
  24.4 15.0 %all-gather.9.cloned.1.call-done = bf16[2048,256]{1,0:T(8,128)(2,1)} async-done(((bf16[512,256]{1,0:T(8,128)(2,1)}), bf16[2048,256]{1,0:T(8,128)(2,1)}) %all-gather.9.cloned.1.call-update) | async-done | bytes 1048592 | tf_op jit(solution)/shard_map/all_gather | solution.py:17
  39.4 4.9 fusion.8
  44.4 0.6 copy-done.25
  45.2 110.1 %reduce-scatter.9.cloned.1.call-done = f32[512,3,256]{2,0,1:T(8,128)} async-done(((f32[2048,3,256]{2,0,1:T(8,128)}), f32[512,3,256]{2,0,1:T(8,128)}) %reduce-scatter.9.cloned.1.call-update) | async-done | bytes 1572880 | tf_op jit(solution)/shard_map/reduce_scatter | solution.py:29
  155.3 1.3 fusion.26
  156.6 3.4 collective-permute-start
  160.0 1.2 collective-permute-done
  161.3 2.2 multiply_convert_fusion.7
  163.5 29.4 %all-gather.11.cloned.1.call-done = bf16[2048,256]{1,0:T(8,128)(2,1)} async-done(((bf16[512,256]{1,0:T(8,128)(2,1)}), bf16[2048,256]{1,0:T(8,128)(2,1)}) %all-gather.11.cloned.1.call-update) | async-done | bytes 1048592 | tf_op jit(solution)/shard_map/all_gather | solution.py:21
  192.9 3.0 fusion.38
  196.0 0.5 all-gather.17.cloned.1.call-update
  196.6 30.1 %reduce-scatter.11.cloned.1.call-done = f32[512,256]{1,0:T(8,128)} async-done(((f32[2048,256]{1,0:T(8,128)}), f32[512,256]{1,0:T(8,128)}) %reduce-scatter.11.cloned.1.call-update) | async-done | bytes 524304 | tf_op jit(solution)/shard_map/reduce_scatter | solution.py:39
  226.7 1.2 multiply_reduce_fusion.5
  227.8 11.7 psum.85
  239.5 0.8 multiply_convert_fusion.6
  240.5 4.3 all-gather.17.cloned.1.call-done
  244.8 6.5 fusion.40
  251.3 12.2 all-gather.13.cloned.1.call-done
  263.5 11.0 fusion.4
  274.6 152.5 %reduce-scatter.17.cloned.1.call-done = f32[512,1152]{1,0:T(8,128)} async-done(((f32[2048,1152]{1,0:T(8,128)}), f32[512,1152]{1,0:T(8,128)}) %reduce-scatter.17.cloned.1.call-update) | async-done | bytes 2359312 | tf_op jit(solution)/shard_map/reduce_scatter | solution.py:29
  427.1 317.3 %reduce-scatter.13.cloned.1.call-done = f32[512,2,1152]{2,0,1:T(8,128)} async-done(((f32[2048,2,1152]{2,0,1:T(8,128)}), f32[512,2,1152]{2,0,1:T(8,128)}) %reduce-scatter.13.cloned.1.call-update) | async-done | bytes 4718608 | tf_op jit(solution)/shard_map/reduce_scatter | solution.py:29
  744.4 5.4 fusion.1
  749.8 1.6 pad_maximum_fusion
  751.5 0.5 all-gather.15.cloned.1.call-update
  752.1 167.2 %all-gather.19.cloned.1.call-done = bf16[2048,2,1152]{2,0,1:T(8,128)(2,1)} async-done(((bf16[512,2,1152]{2,0,1:T(8,128)(2,1)}), bf16[2048,2,1152]{2,0,1:T(8,128)(2,1)}) %all-gather.19.cloned.1.call-update) | async-done | bytes 9437200 | tf_op jit(solution)/shard_map/all_gather | solution.py:21
  919.3 7.7 convolution_bitcast_fusion.1
  927.0 0.2 reduce-scatter.15.cloned.1.call-start
  927.2 81.7 %all-gather.15.cloned.1.call-done = bf16[2048,1152]{1,0:T(8,128)(2,1)} async-done(((bf16[512,1152]{1,0:T(8,128)(2,1)}), bf16[2048,1152]{1,0:T(8,128)(2,1)}) %all-gather.15.cloned.1.call-update) | async-done | bytes 4718608 | tf_op jit(solution)/shard_map/all_gather | solution.py:21
  1008.9 5.2 fusion.39
  1014.2 27.4 %reduce-scatter.19.cloned.1.call-done = f32[512,256]{1,0:T(8,128)} async-done(((f32[2048,256]{1,0:T(8,128)}), f32[512,256]{1,0:T(8,128)}) %reduce-scatter.19.cloned.1.call-update) | async-done | bytes 524304 | tf_op jit(solution)/shard_map/reduce_scatter | solution.py:39
  1041.6 1.8 multiply_reduce_fusion.3
  1043.5 11.7 psum.86
  1055.1 20.1 %reduce-scatter.15.cloned.1.call-done = f32[512,256]{1,0:T(8,128)} async-done(((f32[2048,256]{1,0:T(8,128)}), f32[512,256]{1,0:T(8,128)}) %reduce-scatter.15.cloned.1.call-update) | async-done | bytes 524304 | tf_op jit(solution)/shard_map/reduce_scatter | solution.py:39
  1075.2 2.4 fusion.34
  1077.8 16.8 %all-gather.21.cloned.1.call-done = bf16[2048,256]{1,0:T(8,128)(2,1)} async-done(((bf16[512,256]{1,0:T(8,128)(2,1)}), bf16[2048,256]{1,0:T(8,128)(2,1)}) %all-gather.21.cloned.1.call-update) | async-done | bytes 1048592 | tf_op jit(solution)/shard_map/all_gather | solution.py:17
  1094.6 3.0 fusion.41
  1097.6 43.7 %reduce-scatter.21.cloned.1.call-done = f32[512,256]{1,0:T(8,128)} async-done(((f32[2048,256]{1,0:T(8,128)}), f32[512,256]{1,0:T(8,128)}) %reduce-scatter.21.cloned.1.call-update) | async-done | bytes 524304 | tf_op jit(solution)/shard_map/reduce_scatter | solution.py:29
  1141.4 1.4 multiply_reduce_fusion.1
  1142.8 0.2 multiply_multiply_fusion.2
  1143.0 1.3 collective-permute-start.1
  1144.4 4.1 collective-permute-done.1
  1148.8 1.0 pad_maximum_fusion.1
  1149.8 62.7 %all-gather.23.cloned.1.call-done = bf16[2048,3,256]{2,0,1:T(8,128)(2,1)} async-done(((bf16[512,3,256]{2,0,1:T(8,128)(2,1)}), bf16[2048,3,256]{2,0,1:T(8,128)(2,1)}) %all-gather.23.cloned.1.call-update) | async-done | bytes 3145744 | tf_op jit(solution)/shard_map/all_gather | solution.py:21
  1212.6 4.3 convolution_bitcast_fusion
  1217.0 4.9 fusion.43
  1221.8 8.5 fusion.2
  1230.4 1.2 fusion.42
  1231.6 1.9 fusion.6
  1233.6 13.3 reduce-scatter.23.cloned.1.call-done
  1246.9 1.3 fusion.23
  1248.2 11.7 psum.87
  1259.9 57.6 %all-reduce.1 = (f32[2,1024]{1,0:T(2,128)S(1)}, f32[3,1024]{1,0:T(4,128)S(1)}) all-reduce(f32[2,1024]{1,0:T(2,128)S(1)} %maximum_dynamic-update-slice_fusion.1, f32[3,1024]{1,0:T(4,128)S(1)} %maximum_dynamic-update-slice_fusion), channel_id=1, replica_groups=mesh['dp'=2,'row'=4,'col'=4] {'row','col'}, use_global_device_ids=true, to_apply=%region_18.0 | all-reduce | flops 5120 | bytes 40960 | tf_op jit(solution)/shard_map/psum | solution.py:165
  1317.5 5.9 all-reduce.2
  1323.4 0.6 fusion.37
  1324.0 2.1 fusion.20
  1326.1 41.0 %all-reduce.6.cloned.1.call-done = (f32[256,3,256]{2,0,1:T(8,128)}, f32[256,256]{1,0:T(8,128)}, f32[256,2,1152]{2,0,1:T(8,128)}, f32[1152,256]{1,0:T(8,128)}) async-done(((f32[256,3,256]{2,0,1:T(8,128)}, f32[256,256]{1,0:T(8,128)}, f32[256,2,1152]{2,0,1:T(8,128)}, f32[1152,256]{1,0:T(8,128)}), (f32[256,3,256]{2,0,1:T(8,128)}, f32[256,256]{1,0:T(8,128)}, f32[256,2,1152]{2,0,1:T(8,128)}, ...) | async-done | bytes 4587536 | tf_op jit(solution)/shard_map/psum | solution.py:168
  1367.1 5.0 copy.23
  1372.2 0.9 copy.38
  1373.1 0.7 copy.39
  1373.8 1.0 copy.40
  (111 shorter events, 1.6 us)
Async XLA Ops:
  7.2 256.3 %copy-start = (bf16[256,2,1152]{2,1,0:T(2,128)(2,1)S(1)}, bf16[256,2,1152]{2,1,0:T(2,128)(2,1)}, u32[]{:S(2)}) copy-start(bf16[256,2,1152]{2,1,0:T(2,128)(2,1)} %param.17) | copy-start | bytes 3538948
  7.2 32.2 %all-gather.9.cloned.1.call-start = ((), (), s32[]{:S(2)}) async-start(), calls=%async_computation.8 | async-start | bytes 1310720 | tf_op jit(solution)/shard_map/all_gather | solution.py:17
  24.3 131.0 %reduce-scatter.9.cloned.1.call-start = ((), (), s32[]{:S(2)}) async-start(), calls=%async_computation.9 | async-start | bytes 7864320 | tf_op jit(solution)/shard_map/reduce_scatter | solution.py:29
  44.3 0.7 copy-start.25
  44.3 115.6 %copy-start.29 = (f32[3,256]{1,0:T(4,128)S(1)}, f32[3,256]{1,0:T(4,128)}, u32[]{:S(2)}) copy-start(f32[3,256]{1,0:T(4,128)} %param.14) | copy-start | bytes 9220
  44.4 148.6 %copy-start.16 = (bf16[256,256]{1,0:T(8,128)(2,1)S(1)}, bf16[256,256]{1,0:T(8,128)(2,1)}, u32[]{:S(2)}) copy-start(bf16[256,256]{1,0:T(8,128)(2,1)} %param.15) | copy-start | bytes 393220
  44.4 148.6 %all-gather.11.cloned.1.call-start = ((), (), s32[]{:S(2)}) async-start(), calls=%async_computation.10 | async-start | bytes 1310720 | tf_op jit(solution)/shard_map/all_gather | solution.py:21
  156.6 4.7 collective-permute-start
  160.0 3.4 copy-start.20
  160.0 3.4 copy-start.22
  161.3 2.2 copy-start.26
  163.5 63.2 %copy-start.3 = (bf16[512,256]{1,0:T(8,128)(2,1)S(1)}, bf16[512,256]{1,0:T(8,128)(2,1)}, u32[]{:S(2)}) copy-start(bf16[512,256]{1,0:T(8,128)(2,1)} %param.10) | copy-start | bytes 786436
  163.5 63.2 %reduce-scatter.11.cloned.1.call-start = ((), (), s32[]{:S(2)}) async-start(), calls=%async_computation.11 | async-start | bytes 2621440 | tf_op jit(solution)/shard_map/reduce_scatter | solution.py:39
  195.9 43.6 %copy-start.24 = (f32[256]{0:T(256)S(1)}, f32[256]{0:T(256)}, u32[]{:S(2)}) copy-start(f32[256]{0:T(256)} %param.16) | copy-start | bytes 3076
  195.9 48.9 %copy-start.15 = (bf16[1152,256]{1,0:T(8,128)(2,1)S(1)}, bf16[1152,256]{1,0:T(8,128)(2,1)}, u32[]{:S(2)}) copy-start(bf16[1152,256]{1,0:T(8,128)(2,1)} %param.18) | copy-start | bytes 1769476
  195.9 48.9 %all-gather.17.cloned.1.call-start = ((), (), s32[]{:S(2)}) async-start(), calls=%async_computation.16 | async-start | bytes 1310720 | tf_op jit(solution)/shard_map/all_gather | solution.py:17
  196.5 67.0 %all-gather.13.cloned.1.call-start = ((), (), s32[]{:S(2)}) async-start(), calls=%async_computation.12 | async-start | bytes 1310720 | tf_op jit(solution)/shard_map/all_gather | solution.py:17
  240.4 186.7 %reduce-scatter.17.cloned.1.call-start = ((), (), s32[]{:S(2)}) async-start(), calls=%async_computation.17 | async-start | bytes 11796480 | tf_op jit(solution)/shard_map/reduce_scatter | solution.py:29
  251.3 493.1 %reduce-scatter.13.cloned.1.call-start = ((), (), s32[]{:S(2)}) async-start(), calls=%async_computation.13 | async-start | bytes 23592960 | tf_op jit(solution)/shard_map/reduce_scatter | solution.py:29
  274.5 644.8 %all-gather.19.cloned.1.call-start = ((), (), s32[]{:S(2)}) async-start(), calls=%async_computation.18 | async-start | bytes 11796480 | tf_op jit(solution)/shard_map/all_gather | solution.py:21
  751.4 257.5 %all-gather.15.cloned.1.call-start = ((), (), s32[]{:S(2)}) async-start(), calls=%async_computation.14 | async-start | bytes 5898240 | tf_op jit(solution)/shard_map/all_gather | solution.py:21
  752.0 289.6 %reduce-scatter.19.cloned.1.call-start = ((), (), s32[]{:S(2)}) async-start(), calls=%async_computation.19 | async-start | bytes 2621440 | tf_op jit(solution)/shard_map/reduce_scatter | solution.py:39
  927.0 148.2 %reduce-scatter.15.cloned.1.call-start = ((), (), s32[]{:S(2)}) async-start(), calls=%async_computation.15 | async-start | bytes 2621440 | tf_op jit(solution)/shard_map/reduce_scatter | solution.py:39
  1014.1 61.1 %copy-start.13 = (bf16[512,256]{1,0:T(8,128)(2,1)S(1)}, bf16[512,256]{1,0:T(8,128)(2,1)}, u32[]{:S(2)}) copy-start(bf16[512,256]{1,0:T(8,128)(2,1)} %param.19) | copy-start | bytes 786436
  1014.1 80.4 %copy-start.17 = (bf16[256,256]{1,0:T(8,128)(2,1)S(1)}, bf16[256,256]{1,0:T(8,128)(2,1)}, u32[]{:S(2)}) copy-start(bf16[256,256]{1,0:T(8,128)(2,1)} %param.15) | copy-start | bytes 393220
  1014.1 80.4 %all-gather.21.cloned.1.call-start = ((), (), s32[]{:S(2)}) async-start(), calls=%async_computation.20 | async-start | bytes 1310720 | tf_op jit(solution)/shard_map/all_gather | solution.py:17
  1077.7 63.7 %copy-start.4 = (f32[512,3,256]{2,0,1:T(8,128)S(1)}, f32[512,3,256]{2,0,1:T(8,128)}, u32[]{:S(2)}) copy-start(f32[512,3,256]{2,0,1:T(8,128)} %reduce-scatter.9.cloned.1.call-done) | copy-start | bytes 4718596
  1077.7 63.7 %copy-start.9 = (f32[512,256]{1,0:T(8,128)S(1)}, f32[512,256]{1,0:T(8,128)}, u32[]{:S(2)}) copy-start(f32[512,256]{1,0:T(8,128)} %get-tuple-element.41) | copy-start | bytes 1572868
  1077.7 63.7 %reduce-scatter.21.cloned.1.call-start = ((), (), s32[]{:S(2)}) async-start(), calls=%async_computation.21 | async-start | bytes 2621440 | tf_op jit(solution)/shard_map/reduce_scatter | solution.py:29
  1097.6 45.2 %copy-start.21 = (f32[1,256]{1,0:T(1,128)S(1)}, f32[1,256]{1,0:T(1,128)}, u32[]{:S(2)}) copy-start(f32[1,256]{1,0:T(1,128)} %copy-done.20) | copy-start | bytes 3076
  1097.6 45.2 %copy-start.23 = (f32[1,256]{1,0:T(1,128)S(1)}, f32[1,256]{1,0:T(1,128)}, u32[]{:S(2)}) copy-start(f32[1,256]{1,0:T(1,128)} %copy-done.22) | copy-start | bytes 3076
  1097.6 115.0 %all-gather.23.cloned.1.call-start = ((), (), s32[]{:S(2)}) async-start(), calls=%async_computation.22 | async-start | bytes 3932160 | tf_op jit(solution)/shard_map/all_gather | solution.py:21
  1143.0 5.5 collective-permute-start.1
  1149.7 67.2 %copy-start.11 = (bf16[2048,256]{1,0:T(8,128)(2,1)S(1)}, bf16[2048,256]{1,0:T(8,128)(2,1)}, u32[]{:S(2)}) copy-start(bf16[2048,256]{1,0:T(8,128)(2,1)} %all-gather.17.cloned.1.call-done) | copy-start | bytes 3145732
  1149.8 97.1 %reduce-scatter.23.cloned.1.call-start = ((), (), s32[]{:S(2)}) async-start(), calls=%async_computation.23 | async-start | bytes 2621440 | tf_op jit(solution)/shard_map/reduce_scatter | solution.py:39
  1216.9 4.9 copy-start.2
  1216.9 150.2 %all-reduce.6.cloned.1.call-start = ((), (), s32[]{:S(2)}) async-start(), calls=%async_computation.24 | async-start | bytes 9175040 | tf_op jit(solution)/shard_map/psum | solution.py:168
  1221.8 8.5 copy-start.5
  1221.8 8.5 copy-start.6
  1221.8 9.7 copy-start.8
  1230.4 1.2 copy-start.7
  1233.5 13.4 copy-start.19
  1233.5 26.4 %copy-start.28 = (f32[256]{0:T(256)S(1)}, f32[256]{0:T(256)}, u32[]{:S(2)}) copy-start(f32[256]{0:T(256)} %get-tuple-element.21) | copy-start | bytes 3076
  1233.5 90.5 %copy-start.10 = (f32[512,256]{1,0:T(8,128)S(1)}, f32[512,256]{1,0:T(8,128)}, u32[]{:S(2)}) copy-start(f32[512,256]{1,0:T(8,128)} %get-tuple-element.37) | copy-start | bytes 1572868
  1233.5 90.5 %copy-start.27 = (f32[512]{0:T(512)S(1)}, f32[512]{0:T(512)}, u32[]{:S(2)}) copy-start(f32[512]{0:T(512)} %get-tuple-element.56) | copy-start | bytes 6148
  1367.1 5.1 copy-start.14
  1367.1 5.9 copy-start.18
  1367.1 6.6 copy-start.12
  1367.1 7.6 copy-start.1
Sparse Core Ops, SparseCore 0:
  24.5 14.8 all-gather.8
  44.5 110.7 reduce-scatter.8
  163.6 29.2 all-gather.10
  196.1 30.5 reduce-scatter.10
  228.1 16.6 all-gather.16
  246.8 16.6 all-gather.12
  265.9 161.1 reduce-scatter.16
  429.4 314.8 reduce-scatter.12
  751.5 167.7 all-gather.18
  921.3 87.5 all-gather.14
  1012.0 29.5 reduce-scatter.18
  1044.0 31.1 reduce-scatter.14
  1077.8 16.7 all-gather.20
  1097.7 43.6 reduce-scatter.20
  1149.9 62.6 all-gather.22
  1217.0 29.8 reduce-scatter.22
  1250.5 116.5 all-reduce.5
where the time goes:
time: 1380 us
  waiting for transfers between devices  1150 us (83%)
  blocking collectives  112 us (8%)
  matrix products  62 us (4%)
  other arithmetic  26.7 us (2%)
  between operations  14.3 us (1%)
    reduce_scatter x4, waiting for transfers between devices, summed_rows(): lax.psum_scatter(term(jnp.int32(0), row_count * lax.axis_size('row')), 'r...  624 us
    all_gather x4, waiting for transfers between devices, spread_rows(): return lax.all_gather(local, 'row', axis=0, tiled=True)  341 us
    reduce_scatter x4, waiting for transfers between devices, summed_cols(): lax.psum_scatter(term(jnp.int32(0), row_count * lax.axis_size('col')), 'c...  90.9 us
    psum x1, blocking collectives, on_device(): lax.psum((conv_padded, gain_padded), ('row', 'col'))  57.6 us
    all_gather x4, waiting for transfers between devices, spread_cols(): return lax.all_gather(local, 'col', axis=0, tiled=True)  48.3 us
    dot_general x8, matrix products, term(): jnp.einsum(einsum_form, whole_rows, weight, preferred_element_type=jnp.fl...  45.5 us
    psum x1, waiting for transfers between devices, on_device(): lax.psum((grad_in, grad_out, grad_gate_up, grad_down, conv_own, gain_own)...  41 us
  transfers between devices with their start and end apart: 19, of which 19 were waited for; matrix products, arithmetic and copies ran while one was open for 4% of the time, Pallas kernels for 0%

commit v1 on v0

--- a/solution.py
+++ b/solution.py
@@ -7,6 +7,24 @@
 EPSILON = 1e-05
 
 
+def ring_gather(shard, axis, dim):
+    ways, here, step = (lax.axis_size(axis), lax.axis_index(axis), shard.shape[dim])
+    shape = [n * ways if d == dim else n for d, n in enumerate(shard.shape)]
+    full = lax.dynamic_update_slice_in_dim(
+        jnp.zeros(shape, shard.dtype), shard, here * step, axis=dim
+    )
+    going_up = going_down = shard
+    for far in range(1, ways // 2 + 1):
+        going_up = lax.ppermute(going_up, axis, [(d, (d + 1) % ways) for d in range(ways)])
+        full = lax.dynamic_update_slice_in_dim(full, going_up, (here - far) % ways * step, axis=dim)
+        if 2 * far < ways:
+            going_down = lax.ppermute(going_down, axis, [(d, (d - 1) % ways) for d in range(ways)])
+            full = lax.dynamic_update_slice_in_dim(
+                full, going_down, (here + far) % ways * step, axis=dim
+            )
+    return full
+
+
 def passed_along(block, axis, distance):
     devices = range(lax.axis_size(axis))
     route = [(i - distance, i) for i in devices if i - distance in devices]
@@ -18,7 +36,7 @@
 
 
 def spread_rows(local):
-    return lax.all_gather(local, "row", axis=0, tiled=True)
+    return ring_gather(local, "row", 0)
 
 
 def summed_rows(whole_rows, weight, einsum_form, row_count):

time: 1380 us -> 1320 us (0.957)
  waiting for transfers between devices: 1150 us -> 987 us
  starting transfers between devices: 5.56 us -> 105 us
    all_gather x4 -> x0, waiting for transfers between devices: 341 us -> none  [spread_rows(): return lax.all_gather(local, 'row', axis=0, tiled=True)]
    ppermute x0 -> x12, waiting for transfers between devices: none -> 209 us  [the longest x8 202 us: ring_gather(): lax.ppermute(going_up, axis, [(d, (d + 1) % ways) for d in range(ways)])]
    ppermute x0 -> x12, starting transfers between devices: none -> 99.1 us  [the longest x8 86.9 us: ring_gather(): lax.ppermute(going_up, axis, [(d, (d + 1) % ways) for d in range(ways)])]
    reduce_scatter x4, waiting for transfers between devices: 90.9 us -> 61.8 us  [summed_cols(): lax.psum_scatter(term(jnp.int32(0), row_count * lax.axis_size('col')), 'c...]
  transfers between devices with their start and end apart: 19 -> 27, of which waited for: 19 -> 25; matrix products, arithmetic and copies ran while one was open for 4% -> 4% of each run, Pallas kernels for 0% -> 0%
where the time goes in v1:
time: 1320 us
  waiting for transfers between devices  987 us (75%)
  blocking collectives  109 us (8%)
  starting transfers between devices  105 us (8%)
  matrix products  52.8 us (4%)
  other arithmetic  29.1 us (2%)
  local copies, waits for them, and re-layouts  22.3 us (2%)
  between operations  14.4 us (1%)
    reduce_scatter x4, waiting for transfers between devices, summed_rows(): lax.psum_scatter(term(jnp.int32(0), row_count * lax.axis_size('row')), 'r...  624 us
    ppermute x8, waiting for transfers between devices, ring_gather(): lax.ppermute(going_up, axis, [(d, (d + 1) % ways) for d in range(ways)])  202 us
    ppermute x8, starting transfers between devices, ring_gather(): lax.ppermute(going_up, axis, [(d, (d + 1) % ways) for d in range(ways)])  86.9 us
    reduce_scatter x4, waiting for transfers between devices, summed_cols(): lax.psum_scatter(term(jnp.int32(0), row_count * lax.axis_size('col')), 'c...  61.8 us
    psum x1, blocking collectives, on_device(): lax.psum((conv_padded, gain_padded), ('row', 'col'))  57.6 us
    all_gather x4, waiting for transfers between devices, spread_cols(): return lax.all_gather(local, 'col', axis=0, tiled=True)  45.7 us
    psum x1, waiting for transfers between devices, on_device(): lax.psum((grad_in, grad_out, grad_gate_up, grad_down, conv_own, gain_own)...  41.2 us
    dot_general x8, matrix products, term(): jnp.einsum(einsum_form, whole_rows, weight, preferred_element_type=jnp.fl...  36.6 us
  transfers between devices with their start and end apart: 27, of which 25 were waited for; matrix products, arithmetic and copies ran while one was open for 4% of the time, Pallas kernels for 0%

profile of v1, /device:TPU:0, one launch (start us, length us, event | category | flops | bytes accessed | tf_op | source)
XLA Modules:
  0.0 1319.3 jit_solution(18166730228772591350)
XLA Ops:
  8.4 13.5 %psum.84 = f32[512]{0:T(512)S(1)} all-reduce(f32[512]{0:T(512)S(1)} %fusion.15), channel_id=1, replica_groups=mesh['dp'=2,'row'=4,'col'=4] {'row'}, use_global_device_ids=true, to_apply=%region_1.0 | all-reduce | flops 512 | bytes 4096 | tf_op jit(solution)/shard_map/psum | solution.py:63
  22.5 1.8 fusion.17
  24.4 15.0 %all-gather.5.cloned.1.call-done = bf16[2048,256]{1,0:T(8,128)(2,1)} async-done(((bf16[512,256]{1,0:T(8,128)(2,1)}), bf16[2048,256]{1,0:T(8,128)(2,1)}) %all-gather.5.cloned.1.call-update) | async-done | bytes 1048592 | tf_op jit(solution)/shard_map/all_gather | solution.py:35
  39.4 5.0 fusion.8
  45.2 110.1 %reduce-scatter.9.cloned.1.call-done = f32[512,3,256]{2,0,1:T(8,128)} async-done(((f32[2048,3,256]{2,0,1:T(8,128)}), f32[512,3,256]{2,0,1:T(8,128)}) %reduce-scatter.9.cloned.1.call-update) | async-done | bytes 1572880 | tf_op jit(solution)/shard_map/reduce_scatter | solution.py:47
  156.6 3.4 collective-permute-start
  161.4 2.1 constant_dynamic-update-slice_fusion.17
  163.5 2.3 collective-permute-start.1
  165.8 1.5 collective-permute-start.2
  167.3 7.2 collective-permute-done.1
  174.5 2.9 collective-permute-start.3
  177.5 2.7 collective-permute-done.2
  181.1 2.7 collective-permute-done.3
  184.8 1.8 fusion.38
  187.2 30.8 %reduce-scatter.11.cloned.1.call-done = f32[512,256]{1,0:T(8,128)} async-done(((f32[2048,256]{1,0:T(8,128)}), f32[512,256]{1,0:T(8,128)}) %reduce-scatter.11.cloned.1.call-update) | async-done | bytes 524304 | tf_op jit(solution)/shard_map/reduce_scatter | solution.py:57
  219.2 12.3 psum.85
  232.7 1.5 multiply_convert_fusion.6
  234.3 1.8 all-gather.9.cloned.1.call-done
  236.2 6.6 fusion.40
  242.8 12.1 all-gather.7.cloned.1.call-done
  254.9 11.0 fusion.4
  265.9 152.4 %reduce-scatter.17.cloned.1.call-done = f32[512,1152]{1,0:T(8,128)} async-done(((f32[2048,1152]{1,0:T(8,128)}), f32[512,1152]{1,0:T(8,128)}) %reduce-scatter.17.cloned.1.call-update) | async-done | bytes 2359312 | tf_op jit(solution)/shard_map/reduce_scatter | solution.py:47
  418.3 317.3 %reduce-scatter.13.cloned.1.call-done = f32[512,2,1152]{2,0,1:T(8,128)} async-done(((f32[2048,2,1152]{2,0,1:T(8,128)}), f32[512,2,1152]{2,0,1:T(8,128)}) %reduce-scatter.13.cloned.1.call-update) | async-done | bytes 4718608 | tf_op jit(solution)/shard_map/reduce_scatter | solution.py:47
  735.6 4.2 fusion.1
  741.2 3.7 collective-permute-start.8
  744.8 52.1 %collective-permute-done.7 = bf16[512,2,1152]{2,0,1:T(8,128)(2,1)S(1)} collective-permute-done((bf16[512,2,1152]{2,0,1:T(8,128)(2,1)S(1)}, bf16[512,2,1152]{2,0,1:T(8,128)(2,1)S(1)}, u32[]{:S(2)}, u32[]{:S(2)}) %collective-permute-start.7) | collective-permute-done | bytes 2359328 | tf_op jit(solution)/shard_map/ppermute | solution.py:18
  797.0 49.0 %collective-permute-start.9 = (bf16[512,2,1152]{2,0,1:T(8,128)(2,1)S(1)}, bf16[512,2,1152]{2,0,1:T(8,128)(2,1)S(1)}, u32[]{:S(2)}, u32[]{:S(2)}) collective-permute-start(bf16[512,2,1152]{2,0,1:T(8,128)(2,1)S(1)} %collective-permute-done.7), channel_id=1, source_target_pairs={{0,4},{4,8},{8,12},{12,0},{1,5},{5,9},{9,13},{13,1},{2,6},{6,10},{... | collective-permute-start | bytes 7077896 | tf_op jit(solution)/shard_map/ppermute | solution.py:18
  846.7 51.5 %collective-permute-done.9 = bf16[512,2,1152]{2,0,1:T(8,128)(2,1)S(1)} collective-permute-done((bf16[512,2,1152]{2,0,1:T(8,128)(2,1)S(1)}, bf16[512,2,1152]{2,0,1:T(8,128)(2,1)S(1)}, u32[]{:S(2)}, u32[]{:S(2)}) %collective-permute-start.9) | collective-permute-done | bytes 2359328 | tf_op jit(solution)/shard_map/ppermute | solution.py:18
  898.6 3.6 copy-done.2
  902.2 4.1 convolution_bitcast_fusion.1
  906.8 3.1 constant_dynamic-update-slice_fusion.13
  909.9 3.8 collective-permute-start.5
  913.7 26.8 %collective-permute-done.4 = bf16[512,1152]{1,0:T(8,128)(2,1)S(1)} collective-permute-done((bf16[512,1152]{1,0:T(8,128)(2,1)S(1)}, bf16[512,1152]{1,0:T(8,128)(2,1)S(1)}, u32[]{:S(2)}, u32[]{:S(2)}) %collective-permute-start.4) | collective-permute-done | bytes 1179680 | tf_op jit(solution)/shard_map/ppermute | solution.py:18
  940.6 20.1 %collective-permute-start.6 = (bf16[512,1152]{1,0:T(8,128)(2,1)S(1)}, bf16[512,1152]{1,0:T(8,128)(2,1)S(1)}, u32[]{:S(2)}, u32[]{:S(2)}) collective-permute-start(bf16[512,1152]{1,0:T(8,128)(2,1)S(1)} %collective-permute-done.4), channel_id=1, source_target_pairs={{0,4},{4,8},{8,12},{12,0},{1,5},{5,9},{9,13},{13,1},{2,6},{6,10},{... | collective-permute-start | bytes 3538952 | tf_op jit(solution)/shard_map/ppermute | solution.py:18
  960.8 1.5 collective-permute-done.5
  962.5 26.2 %collective-permute-done.6 = bf16[512,1152]{1,0:T(8,128)(2,1)S(1)} collective-permute-done((bf16[512,1152]{1,0:T(8,128)(2,1)S(1)}, bf16[512,1152]{1,0:T(8,128)(2,1)S(1)}, u32[]{:S(2)}, u32[]{:S(2)}) %collective-permute-start.6) | collective-permute-done | bytes 1179680 | tf_op jit(solution)/shard_map/ppermute | solution.py:18
  988.9 2.2 copy-done.8
  991.1 2.8 fusion.39
  994.1 1.9 multiply_reduce_fusion.3
  995.9 8.3 psum.86
  1004.3 18.8 %reduce-scatter.15.cloned.1.call-done = f32[512,256]{1,0:T(8,128)} async-done(((f32[2048,256]{1,0:T(8,128)}), f32[512,256]{1,0:T(8,128)}) %reduce-scatter.15.cloned.1.call-update) | async-done | bytes 524304 | tf_op jit(solution)/shard_map/reduce_scatter | solution.py:57
  1023.1 2.4 fusion.34
  1025.7 16.8 %all-gather.11.cloned.1.call-done = bf16[2048,256]{1,0:T(8,128)(2,1)} async-done(((bf16[512,256]{1,0:T(8,128)(2,1)}), bf16[2048,256]{1,0:T(8,128)(2,1)}) %all-gather.11.cloned.1.call-update) | async-done | bytes 1048592 | tf_op jit(solution)/shard_map/all_gather | solution.py:35
  1042.4 3.0 fusion.41
  1045.5 43.7 %reduce-scatter.21.cloned.1.call-done = f32[512,256]{1,0:T(8,128)} async-done(((f32[2048,256]{1,0:T(8,128)}), f32[512,256]{1,0:T(8,128)}) %reduce-scatter.21.cloned.1.call-update) | async-done | bytes 524304 | tf_op jit(solution)/shard_map/reduce_scatter | solution.py:47
  1089.3 2.1 multiply_reduce_fusion.1
  1093.1 4.1 collective-permute-done.10
  1098.5 3.2 collective-permute-start.12
  1101.7 18.4 %collective-permute-done.11 = bf16[512,3,256]{2,0,1:T(8,128)(2,1)S(1)} collective-permute-done((bf16[512,3,256]{2,0,1:T(8,128)(2,1)S(1)}, bf16[512,3,256]{2,0,1:T(8,128)(2,1)S(1)}, u32[]{:S(2)}, u32[]{:S(2)}) %collective-permute-start.11) | collective-permute-done | bytes 786464 | tf_op jit(solution)/shard_map/ppermute | solution.py:18
  1120.1 11.6 collective-permute-start.13
  1131.7 2.5 collective-permute-done.12
  1134.3 16.9 %collective-permute-done.13 = bf16[512,3,256]{2,0,1:T(8,128)(2,1)S(1)} collective-permute-done((bf16[512,3,256]{2,0,1:T(8,128)(2,1)S(1)}, bf16[512,3,256]{2,0,1:T(8,128)(2,1)S(1)}, u32[]{:S(2)}, u32[]{:S(2)}) %collective-permute-start.13) | collective-permute-done | bytes 786464 | tf_op jit(solution)/shard_map/ppermute | solution.py:18
  1151.2 1.6 copy-done.3
  1152.8 2.4 convolution_bitcast_fusion
  1155.5 4.8 fusion.43
  1160.3 8.3 fusion.2
  1169.9 1.9 fusion.6
  1172.5 12.2 reduce-scatter.23.cloned.1.call-done
  1186.0 11.7 psum.87
  1197.7 57.6 %all-reduce.1 = (f32[2,1024]{1,0:T(2,128)S(1)}, f32[3,1024]{1,0:T(4,128)S(1)}) all-reduce(f32[2,1024]{1,0:T(2,128)S(1)} %constant_dynamic-update-slice_fusion.1, f32[3,1024]{1,0:T(4,128)S(1)} %constant_dynamic-update-slice_fusion), channel_id=1, replica_groups=mesh['dp'=2,'row'=4,'col'=4] {'row','col'}, use_global_device_ids=true, to_apply=%region_18.19 | all-reduce | flops 5120 | bytes 40960 | tf_op jit(solution)/shard_map/psum | solution.py:183
  1255.4 5.9 all-reduce.2
  1261.8 2.1 fusion.20
  1263.9 41.2 %all-reduce.6.cloned.1.call-done = (f32[256,3,256]{2,0,1:T(8,128)}, f32[256,256]{1,0:T(8,128)}, f32[256,2,1152]{2,0,1:T(8,128)}, f32[1152,256]{1,0:T(8,128)}) async-done(((f32[256,3,256]{2,0,1:T(8,128)}, f32[256,256]{1,0:T(8,128)}, f32[256,2,1152]{2,0,1:T(8,128)}, f32[1152,256]{1,0:T(8,128)}), (f32[256,3,256]{2,0,1:T(8,128)}, f32[256,256]{1,0:T(8,128)}, f32[256,2,1152]{2,0,1:T(8,128)}, ...) | async-done | bytes 4587536 | tf_op jit(solution)/shard_map/psum | solution.py:186
  1305.1 5.0 copy.23
  (160 shorter events, 24.1 us)
Async XLA Ops:
  7.2 247.7 %copy-start = (bf16[256,2,1152]{2,1,0:T(2,128)(2,1)S(1)}, bf16[256,2,1152]{2,1,0:T(2,128)(2,1)}, u32[]{:S(2)}) copy-start(bf16[256,2,1152]{2,1,0:T(2,128)(2,1)} %param.17) | copy-start | bytes 3538948
  7.2 32.2 %all-gather.5.cloned.1.call-start = ((), (), s32[]{:S(2)}) async-start(), calls=%async_computation.8 | async-start | bytes 1310720 | tf_op jit(solution)/shard_map/all_gather | solution.py:35
  24.3 131.0 %reduce-scatter.9.cloned.1.call-start = ((), (), s32[]{:S(2)}) async-start(), calls=%async_computation.9 | async-start | bytes 7864320 | tf_op jit(solution)/shard_map/reduce_scatter | solution.py:47
  44.3 115.6 %copy-start.39 = (f32[3,256]{1,0:T(4,128)S(1)}, f32[3,256]{1,0:T(4,128)}, u32[]{:S(2)}) copy-start(f32[3,256]{1,0:T(4,128)} %param.14) | copy-start | bytes 9220
  44.4 173.6 %reduce-scatter.11.cloned.1.call-start = ((), (), s32[]{:S(2)}) async-start(), calls=%async_computation.10 | async-start | bytes 2621440 | tf_op jit(solution)/shard_map/reduce_scatter | solution.py:57
  156.6 4.7 collective-permute-start
  160.0 3.5 copy-start.25
  160.0 3.4 copy-start.27
  160.0 24.8 %copy-start.23 = (f32[1,256]{1,0:T(1,128)}, f32[1,256]{1,0:T(1,128)S(1)}, u32[]{:S(2)}) copy-start(f32[1,256]{1,0:T(1,128)S(1)} %get-tuple-element.55) | copy-start | bytes 3076
  161.3 2.2 copy-start.33
  161.3 23.5 %copy-start.18 = (bf16[256,256]{1,0:T(8,128)(2,1)S(1)}, bf16[256,256]{1,0:T(8,128)(2,1)}, u32[]{:S(2)}) copy-start(bf16[256,256]{1,0:T(8,128)(2,1)} %param.15) | copy-start | bytes 393220
  163.5 11.1 collective-permute-start.1
  165.8 14.4 %collective-permute-start.2 = (bf16[512,256]{1,0:T(8,128)(2,1)S(1)}, bf16[512,256]{1,0:T(8,128)(2,1)}, u32[]{:S(2)}, u32[]{:S(2)}) collective-permute-start(bf16[512,256]{1,0:T(8,128)(2,1)S(1)} %get-tuple-element.43), channel_id=1, source_target_pairs={{0,12},{4,0},{8,4},{12,8},{1,13},{5,1},{9,5},{13,9},{2,14},{6,2},{... | collective-permute-start | bytes 786440 | tf_op jit(solution)/shard_map/ppermute | solution.py:21
  174.5 9.3 collective-permute-start.3
  184.8 33.2 %copy-start.6 = (bf16[512,256]{1,0:T(8,128)(2,1)S(1)}, bf16[512,256]{1,0:T(8,128)(2,1)}, u32[]{:S(2)}) copy-start(bf16[512,256]{1,0:T(8,128)(2,1)} %param.10) | copy-start | bytes 786436
  186.6 49.5 %all-gather.9.cloned.1.call-start = ((), (), s32[]{:S(2)}) async-start(), calls=%async_computation.14 | async-start | bytes 1310720 | tf_op jit(solution)/shard_map/all_gather | solution.py:35
  187.2 67.7 %all-gather.7.cloned.1.call-start = ((), (), s32[]{:S(2)}) async-start(), calls=%async_computation.11 | async-start | bytes 1310720 | tf_op jit(solution)/shard_map/all_gather | solution.py:35
  234.3 184.0 %reduce-scatter.17.cloned.1.call-start = ((), (), s32[]{:S(2)}) async-start(), calls=%async_computation.15 | async-start | bytes 11796480 | tf_op jit(solution)/shard_map/reduce_scatter | solution.py:47
  242.8 492.8 %reduce-scatter.13.cloned.1.call-start = ((), (), s32[]{:S(2)}) async-start(), calls=%async_computation.12 | async-start | bytes 23592960 | tf_op jit(solution)/shard_map/reduce_scatter | solution.py:47
  265.9 728.2 %reduce-scatter.19.cloned.1.call-start = ((), (), s32[]{:S(2)}) async-start(), calls=%async_computation.16 | async-start | bytes 2621440 | tf_op jit(solution)/shard_map/reduce_scatter | solution.py:57
  741.0 56.0 %collective-permute-start.7 = (bf16[512,2,1152]{2,0,1:T(8,128)(2,1)S(1)}, bf16[512,2,1152]{2,0,1:T(8,128)(2,1)S(1)}, u32[]{:S(2)}, u32[]{:S(2)}) collective-permute-start(bf16[512,2,1152]{2,0,1:T(8,128)(2,1)S(1)} %get-tuple-element.47), channel_id=1, source_target_pairs={{0,4},{4,8},{8,12},{12,0},{1,5},{5,9},{9,13},{13,1},{2,6},{6,10},{... | collective-permute-start | bytes 7077896 | tf_op jit(solution)/shard_map/ppermute | solution.py:18
  741.2 105.2 %collective-permute-start.8 = (bf16[512,2,1152]{2,0,1:T(8,128)(2,1)S(1)}, bf16[512,2,1152]{2,0,1:T(8,128)(2,1)S(1)}, u32[]{:S(2)}, u32[]{:S(2)}) collective-permute-start(bf16[512,2,1152]{2,0,1:T(8,128)(2,1)S(1)} %get-tuple-element.47), channel_id=1, source_target_pairs={{0,12},{4,0},{8,4},{12,8},{1,13},{5,1},{9,5},{13,9},{2,14},{6,2},{... | collective-permute-start | bytes 7077896 | tf_op jit(solution)/shard_map/ppermute | solution.py:21
  797.0 101.3 %collective-permute-start.9 = (bf16[512,2,1152]{2,0,1:T(8,128)(2,1)S(1)}, bf16[512,2,1152]{2,0,1:T(8,128)(2,1)S(1)}, u32[]{:S(2)}, u32[]{:S(2)}) collective-permute-start(bf16[512,2,1152]{2,0,1:T(8,128)(2,1)S(1)} %collective-permute-done.7), channel_id=1, source_target_pairs={{0,4},{4,8},{8,12},{12,0},{1,5},{5,9},{9,13},{13,1},{2,6},{6,10},{... | collective-permute-start | bytes 7077896 | tf_op jit(solution)/shard_map/ppermute | solution.py:18
  898.6 3.6 copy-start.2
  906.4 116.8 %reduce-scatter.15.cloned.1.call-start = ((), (), s32[]{:S(2)}) async-start(), calls=%async_computation.13 | async-start | bytes 2621440 | tf_op jit(solution)/shard_map/reduce_scatter | solution.py:57
  909.9 30.7 %collective-permute-start.4 = (bf16[512,1152]{1,0:T(8,128)(2,1)S(1)}, bf16[512,1152]{1,0:T(8,128)(2,1)S(1)}, u32[]{:S(2)}, u32[]{:S(2)}) collective-permute-start(bf16[512,1152]{1,0:T(8,128)(2,1)S(1)} %get-tuple-element.39), channel_id=1, source_target_pairs={{0,4},{4,8},{8,12},{12,0},{1,5},{5,9},{9,13},{13,1},{2,6},{6,10},{... | collective-permute-start | bytes 3538952 | tf_op jit(solution)/shard_map/ppermute | solution.py:18
  909.9 52.4 %collective-permute-start.5 = (bf16[512,1152]{1,0:T(8,128)(2,1)S(1)}, bf16[512,1152]{1,0:T(8,128)(2,1)S(1)}, u32[]{:S(2)}, u32[]{:S(2)}) collective-permute-start(bf16[512,1152]{1,0:T(8,128)(2,1)S(1)} %get-tuple-element.39), channel_id=1, source_target_pairs={{0,12},{4,0},{8,4},{12,8},{1,13},{5,1},{9,5},{13,9},{2,14},{6,2},{... | collective-permute-start | bytes 3538952 | tf_op jit(solution)/shard_map/ppermute | solution.py:21
  940.6 48.1 %collective-permute-start.6 = (bf16[512,1152]{1,0:T(8,128)(2,1)S(1)}, bf16[512,1152]{1,0:T(8,128)(2,1)S(1)}, u32[]{:S(2)}, u32[]{:S(2)}) collective-permute-start(bf16[512,1152]{1,0:T(8,128)(2,1)S(1)} %collective-permute-done.4), channel_id=1, source_target_pairs={{0,4},{4,8},{8,12},{12,0},{1,5},{5,9},{9,13},{13,1},{2,6},{6,10},{... | collective-permute-start | bytes 3538952 | tf_op jit(solution)/shard_map/ppermute | solution.py:18
  960.8 30.3 %copy-start.17 = (bf16[1152,256]{1,0:T(8,128)(2,1)S(1)}, bf16[1152,256]{1,0:T(8,128)(2,1)}, u32[]{:S(2)}) copy-start(bf16[1152,256]{1,0:T(8,128)(2,1)} %param.18) | copy-start | bytes 1769476
  988.9 2.2 copy-start.8
  991.1 3.0 copy-start.29
  993.9 29.2 %copy-start.15 = (bf16[512,256]{1,0:T(8,128)(2,1)S(1)}, bf16[512,256]{1,0:T(8,128)(2,1)}, u32[]{:S(2)}) copy-start(bf16[512,256]{1,0:T(8,128)(2,1)} %param.19) | copy-start | bytes 786436
  993.9 29.2 %copy-start.30 = (f32[512]{0:T(512)S(1)}, f32[512]{0:T(512)}, u32[]{:S(2)}) copy-start(f32[512]{0:T(512)} %get-tuple-element.64) | copy-start | bytes 6148
  994.0 48.5 %copy-start.19 = (bf16[256,256]{1,0:T(8,128)(2,1)S(1)}, bf16[256,256]{1,0:T(8,128)(2,1)}, u32[]{:S(2)}) copy-start(bf16[256,256]{1,0:T(8,128)(2,1)} %param.15) | copy-start | bytes 393220
  994.0 48.5 %all-gather.11.cloned.1.call-start = ((), (), s32[]{:S(2)}) async-start(), calls=%async_computation.17 | async-start | bytes 1310720 | tf_op jit(solution)/shard_map/all_gather | solution.py:35
  1025.6 63.7 %copy-start.11 = (f32[512,256]{1,0:T(8,128)S(1)}, f32[512,256]{1,0:T(8,128)}, u32[]{:S(2)}) copy-start(f32[512,256]{1,0:T(8,128)} %get-tuple-element.44) | copy-start | bytes 1572868
  1025.6 63.7 %copy-start.34 = (f32[2,256]{1,0:T(2,128)S(1)}, f32[2,256]{1,0:T(2,128)}, u32[]{:S(2)}) copy-start(f32[2,256]{1,0:T(2,128)} %copy-done.33) | copy-start | bytes 6148
  1025.6 63.7 %reduce-scatter.21.cloned.1.call-start = ((), (), s32[]{:S(2)}) async-start(), calls=%async_computation.18 | async-start | bytes 2621440 | tf_op jit(solution)/shard_map/reduce_scatter | solution.py:47
  1045.5 45.9 %copy-start.26 = (f32[1,256]{1,0:T(1,128)S(1)}, f32[1,256]{1,0:T(1,128)}, u32[]{:S(2)}) copy-start(f32[1,256]{1,0:T(1,128)} %copy-done.25) | copy-start | bytes 3076
  1045.5 45.9 %copy-start.28 = (f32[1,256]{1,0:T(1,128)S(1)}, f32[1,256]{1,0:T(1,128)}, u32[]{:S(2)}) copy-start(f32[1,256]{1,0:T(1,128)} %copy-done.27) | copy-start | bytes 3076
  1045.5 139.2 %reduce-scatter.23.cloned.1.call-start = ((), (), s32[]{:S(2)}) async-start(), calls=%async_computation.19 | async-start | bytes 2621440 | tf_op jit(solution)/shard_map/reduce_scatter | solution.py:57
  1091.3 5.9 copy-start.7
  1091.4 5.9 copy-start.24
  1091.6 5.6 collective-permute-start.10
  1097.8 22.3 %collective-permute-start.11 = (bf16[512,3,256]{2,0,1:T(8,128)(2,1)S(1)}, bf16[512,3,256]{2,0,1:T(8,128)(2,1)S(1)}, u32[]{:S(2)}, u32[]{:S(2)}) collective-permute-start(bf16[512,3,256]{2,0,1:T(8,128)(2,1)S(1)} %get-tuple-element.49), channel_id=1, source_target_pairs={{0,4},{4,8},{8,12},{12,0},{1,5},{5,9},{9,13},{13,1},{2,6},{6,10},{... | collective-permute-start | bytes 2359304 | tf_op jit(solution)/shard_map/ppermute | solution.py:18
  1098.5 35.7 %collective-permute-start.12 = (bf16[512,3,256]{2,0,1:T(8,128)(2,1)S(1)}, bf16[512,3,256]{2,0,1:T(8,128)(2,1)S(1)}, u32[]{:S(2)}, u32[]{:S(2)}) collective-permute-start(bf16[512,3,256]{2,0,1:T(8,128)(2,1)S(1)} %get-tuple-element.49), channel_id=1, source_target_pairs={{0,12},{4,0},{8,4},{12,8},{1,13},{5,1},{9,5},{13,9},{2,14},{6,2},{... | collective-permute-start | bytes 2359304 | tf_op jit(solution)/shard_map/ppermute | solution.py:21
  1120.1 31.1 %collective-permute-start.13 = (bf16[512,3,256]{2,0,1:T(8,128)(2,1)S(1)}, bf16[512,3,256]{2,0,1:T(8,128)(2,1)S(1)}, u32[]{:S(2)}, u32[]{:S(2)}) collective-permute-start(bf16[512,3,256]{2,0,1:T(8,128)(2,1)S(1)} %collective-permute-done.11), channel_id=1, source_target_pairs={{0,4},{4,8},{8,12},{12,0},{1,5},{5,9},{9,13},{13,1},{2,6},{6,10},{... | collective-permute-start | bytes 2359304 | tf_op jit(solution)/shard_map/ppermute | solution.py:18
  1131.7 21.2 %copy-start.20 = (bf16[256,3,256]{2,0,1:T(8,128)(2,1)S(1)}, bf16[256,3,256]{2,0,1:T(8,128)(2,1)}, u32[]{:S(2)}) copy-start(bf16[256,3,256]{2,0,1:T(8,128)(2,1)} %param.13) | copy-start | bytes 1179652
  1151.2 1.6 copy-start.3
  1152.8 2.7 copy-start.13
  1155.2 5.1 copy-start.5
  1155.2 149.8 %all-reduce.6.cloned.1.call-start = ((), (), s32[]{:S(2)}) async-start(), calls=%async_computation.20 | async-start | bytes 9175040 | tf_op jit(solution)/shard_map/psum | solution.py:186
  1160.3 8.3 copy-start.9
  1160.3 9.5 copy-start.4
  1168.6 1.2 copy-start.10
  1171.8 0.7 copy-start.37
  1171.8 12.9 copy-start.22
  1171.8 25.9 %copy-start.38 = (f32[256]{0:T(256)S(1)}, f32[256]{0:T(256)}, u32[]{:S(2)}) copy-start(f32[256]{0:T(256)} %get-tuple-element.21) | copy-start | bytes 3076
  1171.8 90.0 %copy-start.12 = (f32[512,256]{1,0:T(8,128)S(1)}, f32[512,256]{1,0:T(8,128)}, u32[]{:S(2)}) copy-start(f32[512,256]{1,0:T(8,128)} %get-tuple-element.37) | copy-start | bytes 1572868
  1171.8 90.0 %copy-start.32 = (f32[512]{0:T(512)S(1)}, f32[512]{0:T(512)}, u32[]{:S(2)}) copy-start(f32[512]{0:T(512)} %get-tuple-element.62) | copy-start | bytes 6148
  1305.1 5.1 copy-start.16
  1305.1 5.9 copy-start.21
  1305.1 6.6 copy-start.14
  1305.1 7.6 copy-start.1
  (3 other events, 2.1 us)
Sparse Core Ops, SparseCore 0:
  24.4 14.8 all-gather.4
  44.5 110.7 reduce-scatter.8
  186.7 31.2 reduce-scatter.10
  219.4 16.6 all-gather.8
  238.1 16.6 all-gather.6
  257.1 161.1 reduce-scatter.16
  420.7 314.8 reduce-scatter.12
  906.5 30.4 reduce-scatter.18
  994.1 28.9 reduce-scatter.14
  1025.7 16.6 all-gather.10
  1045.6 43.6 reduce-scatter.20
  1155.3 29.2 reduce-scatter.22
  1188.5 116.5 all-reduce.5
